TPU v7x, 32 devices: a whole 2x2x4 slice. The times are simulated.
32 devices in a mesh: inb: 4 (over y, x), outb: 8 (over z, core).
Axes of the slice: x: 2, y: 2, z: 4, core: 2. Of those that a mesh axis runs over, the one named last changes fastest.
Arguments:
- site_cores: float32 [2, 4, 8192, 8192], P(None, None, 'inb', 'outb')
- left_env: float32 [512, 8192], P(None, 'outb')
- outcomes: int32 [2, 512], replicated, may hold values from 0 to 3
Outputs:
- env_out: float32 [512, 8192], P('inb', 'outb')
- probabilities: float32 [2, 4, 512], P(None, None, 'inb')
- log_scale: float32 [512], P('inb')
All inputs are finite; a program needn't handle non-finite values.
Results may differ from a plain program's by a relative error of at most 0.00014.
Values sent between devices are 32-bit elements; how exact they have to be, the bound alone decides.
A program may use at most 128 MiB of HBM per device.

v0:
```python
import jax
import jax.numpy as jnp
from jax import lax
from jax.sharding import PartitionSpec as P

epsilon = 1e-06


def on_device(site_cores, left_env, outcomes):
    inb_index = lax.axis_index("inb")
    inb_count = lax.axis_size("inb")
    samples_all = left_env.shape[0]
    block_rows = samples_all // inb_count
    width_out = site_cores.shape[3]
    bond_width = width_out * lax.axis_size("outb")
    outcome_count = site_cores.shape[1]
    levels = jnp.arange(outcome_count, dtype=jnp.int32)
    current = lax.dynamic_slice_in_dim(left_env, inb_index * block_rows, block_rows, 0)
    chosen_ids = lax.dynamic_slice_in_dim(outcomes, inb_index * block_rows, block_rows, 1)
    log_scale = jnp.zeros((chosen_ids.shape[1],), jnp.float32)
    prob_list = []
    for site_index in range(site_cores.shape[0]):
        sample_rows = lax.all_gather(current, "outb", axis=1, tiled=True)
        own_cols = lax.all_to_all(sample_rows, "inb", split_axis=1, concat_axis=0, tiled=True)
        partial_terms = jnp.einsum(
            "sc,pcd->psd", own_cols, site_cores[site_index], precision=lax.Precision.HIGHEST
        )
        candidates = lax.psum_scatter(partial_terms, "inb", scatter_dimension=1, tiled=True)
        squares = jnp.sum(candidates * candidates, axis=2)
        totals = lax.psum(squares, "outb")
        mean_squares = totals / bond_width + epsilon
        prob_list.append(mean_squares / jnp.sum(mean_squares, axis=0, keepdims=True))
        onehot = (chosen_ids[site_index][None, :] == levels[:, None]).astype(jnp.float32)
        chosen = jnp.sum(onehot[:, :, None] * candidates, axis=0)
        chosen_mean = jnp.sum(onehot * mean_squares, axis=0)
        inverse = lax.rsqrt(chosen_mean)
        log_scale = log_scale + 0.5 * jnp.log(chosen_mean)
        current = chosen * inverse[:, None]
    prob_stack = jnp.stack(prob_list)
    return (current, prob_stack, log_scale)


def solution(mesh):
    in_specs = (P(None, None, "inb", "outb"), P(None, "outb"), P())
    out_specs = (P("inb", "outb"), P(None, None, "inb"), P("inb"))
    return jax.shard_map(
        on_device, mesh=mesh, in_specs=in_specs, out_specs=out_specs, check_vma=False
    )
```

profile of v0, /device:TPU:0, one launch (start us, length us, event | category | flops | bytes accessed | tf_op | source)
XLA Modules:
  0.0 555.6 jit_solution(1600820002237552070)
XLA Ops:
  7.2 0.0 copy-start
  7.2 0.0 all-gather.3.cloned.1.call-start
  7.2 1.5 copy-done
  8.8 0.8 constant_dynamic-slice_fusion
  9.6 0.0 all-gather.3.cloned.1.call-update
  9.6 0.0 reduce-scatter.3.cloned.1.call-start
  9.7 50.1 %all-gather.3.cloned.1.call-done = f32[128,8192]{1,0:T(8,128)} async-done(((f32[128,1024]{1,0:T(8,128)}), f32[128,8192]{1,0:T(8,128)}) %all-gather.3.cloned.1.call-update) | async-done | bytes 4194320 | tf_op jit(solution)/shard_map/all_gather | solution.py:23
  59.8 2.5 copy.14
  62.3 51.7 %all_to_all.38 = f32[128,4,2048]{2,0,1:T(8,128)S(1)} all-to-all(f32[128,4,2048]{2,0,1:T(8,128)S(1)} %bitcast.46), channel_id=1, replica_groups=mesh['inb'=4,'outb'=8] {'inb'}, dimensions={1} | all-to-all | bytes 8388608 | tf_op jit(solution)/shard_map/all_to_all | solution.py:24
  113.9 59.2 %fusion.6 = f32[4,512,1024]{2,1,0:T(8,128)} fusion(f32[512,2048,1]{1,0,2:T(8,128)S(1)} %bitcast.50, f32[2,4,2048,1024]{3,2,1,0:T(8,128)} %param.3), kind=kOutput, calls=%fused_computation.7 | convolution fusion | flops 51539607552 | bytes 46137344 | tf_op jit(solution)/shard_map/sc,pcd->psd/dot_general | solution.py:25
  173.2 0.0 reduce-scatter.3.cloned.1.call-update
  173.2 0.2 all-gather.5.cloned.1.call-start
  173.4 0.7 constant_dynamic-slice_fusion.1
  174.1 82.9 %reduce-scatter.3.cloned.1.call-done = f32[4,128,1024]{2,1,0:T(8,128)} async-done(((f32[4,512,1024]{2,1,0:T(8,128)}), f32[4,128,1024]{2,1,0:T(8,128)}) %reduce-scatter.3.cloned.1.call-update) | async-done | bytes 2097168 | tf_op jit(solution)/shard_map/reduce_scatter | solution.py:28
  257.0 2.0 multiply_reduce_fusion.2
  259.0 16.2 %psum.14 = f32[4,128]{1,0:T(4,128)S(1)} all-reduce(f32[4,128]{1,0:T(4,128)S(1)} %get-tuple-element.5), channel_id=1, replica_groups=mesh['inb'=4,'outb'=8] {'outb'}, use_global_device_ids=true, to_apply=%region_3.0 | all-reduce | flops 512 | bytes 4096 | tf_op jit(solution)/shard_map/psum | solution.py:30
  275.2 0.9 broadcast_multiply_fusion.1
  276.1 0.0 all-gather.5.cloned.1.call-update
  276.1 0.0 reduce-scatter.5.cloned.1.call-start
  276.2 44.2 %all-gather.5.cloned.1.call-done = f32[128,8192]{1,0:T(8,128)} async-done(((f32[128,1024]{1,0:T(8,128)}), f32[128,8192]{1,0:T(8,128)}) %all-gather.5.cloned.1.call-update) | async-done | bytes 4194320 | tf_op jit(solution)/shard_map/all_gather | solution.py:23
  320.4 5.6 %copy.10 = f32[128,8192]{0,1:T(8,128)} copy(f32[128,8192]{1,0:T(8,128)} %all-gather.5.cloned.1.call-done) | data formatting | bytes 8388608 | tf_op jit(solution)/shard_map/all_gather | solution.py:23
  326.0 54.2 %all_to_all.39 = f32[128,4,2048]{0,2,1:T(8,128)} all-to-all(f32[128,4,2048]{0,2,1:T(8,128)} %bitcast.47), channel_id=1, replica_groups=mesh['inb'=4,'outb'=8] {'inb'}, dimensions={1} | all-to-all | bytes 8388608 | tf_op jit(solution)/shard_map/all_to_all | solution.py:24
  380.2 5.4 copy.11
  385.6 59.2 %fusion.9 = f32[4,512,1024]{2,1,0:T(8,128)} fusion(f32[512,2048,1]{1,0,2:T(8,128)} %bitcast.51, f32[2,4,2048,1024]{3,2,1,0:T(8,128)} %param.3), kind=kOutput, calls=%fused_computation.8 | convolution fusion | flops 51539607552 | bytes 46137344 | tf_op jit(solution)/shard_map/sc,pcd->psd/dot_general | solution.py:25
  444.9 0.0 reduce-scatter.5.cloned.1.call-update
  444.9 83.9 %reduce-scatter.5.cloned.1.call-done = f32[4,128,1024]{2,1,0:T(8,128)} async-done(((f32[4,512,1024]{2,1,0:T(8,128)}), f32[4,128,1024]{2,1,0:T(8,128)}) %reduce-scatter.5.cloned.1.call-update) | async-done | bytes 2097168 | tf_op jit(solution)/shard_map/reduce_scatter | solution.py:28
  528.8 2.0 multiply_reduce_fusion
  530.8 16.2 %psum.15 = f32[4,128]{1,0:T(4,128)S(1)} all-reduce(f32[4,128]{1,0:T(4,128)S(1)} %get-tuple-element.3), channel_id=1, replica_groups=mesh['inb'=4,'outb'=8] {'outb'}, use_global_device_ids=true, to_apply=%region_8.0 | all-reduce | flops 512 | bytes 4096 | tf_op jit(solution)/shard_map/psum | solution.py:30
  547.1 0.5 add_multiply_fusion
  547.6 0.6 pad_maximum_fusion
  548.2 0.9 broadcast_multiply_fusion
  (8 shorter events, 0.1 us)
Async XLA Ops:
  7.2 1.6 copy-start
  7.2 52.6 %all-gather.3.cloned.1.call-start = ((), (), s32[]{:S(2)}) async-start(), calls=%async_computation.4 | async-start | bytes 4718592 | tf_op jit(solution)/shard_map/all_gather | solution.py:23
  9.6 247.4 %reduce-scatter.3.cloned.1.call-start = ((), (), s32[]{:S(2)}) async-start(), calls=%async_computation.5 | async-start | bytes 10485760 | tf_op jit(solution)/shard_map/reduce_scatter | solution.py:28
  173.2 147.2 %all-gather.5.cloned.1.call-start = ((), (), s32[]{:S(2)}) async-start(), calls=%async_computation.6 | async-start | bytes 4718592 | tf_op jit(solution)/shard_map/all_gather | solution.py:23
  276.1 252.7 %reduce-scatter.5.cloned.1.call-start = ((), (), s32[]{:S(2)}) async-start(), calls=%async_computation.7 | async-start | bytes 10485760 | tf_op jit(solution)/shard_map/reduce_scatter | solution.py:28
Sparse Core Ops, SparseCore 0:
  10.2 49.5 all-gather.2
  173.3 83.6 reduce-scatter.2
  276.3 44.0 all-gather.4
  445.0 83.7 reduce-scatter.4
where the time goes:
time: 556 us
  waiting for transfers between devices  261 us (47%)
  blocking collectives  138 us (25%)
  matrix products  118 us (21%)
  local copies, waits for them, and re-layouts  16.5 us (3%)
  between operations  13.8 us (2%)
  other arithmetic  6.98 us (1%)
    reduce_scatter x2, waiting for transfers between devices, on_device(): lax.psum_scatter(partial_terms, 'inb', scatter_dimension=1, tiled=True)  167 us
    dot_general x2, matrix products, on_device(): jnp.einsum('sc,pcd->psd', own_cols, site_cores[site_index], precision=lax...  118 us
    all_to_all x2, blocking collectives, on_device(): lax.all_to_all(sample_rows, 'inb', split_axis=1, concat_axis=0, tiled=True)  106 us
    all_gather x2, waiting for transfers between devices, on_device(): sample_rows = lax.all_gather(current, 'outb', axis=1, tiled=True)  94.3 us
    psum x2, blocking collectives, on_device(): totals = lax.psum(squares, 'outb')  32.4 us
  transfers between devices with their start and end apart: 4, of which 4 were waited for; matrix products, arithmetic and copies ran while one was open for 0% of the time, Pallas kernels for 0%

commit v1 on v0

--- a/solution.py
+++ b/solution.py
@@ -20,7 +20,14 @@
     log_scale = jnp.zeros((chosen_ids.shape[1],), jnp.float32)
     prob_list = []
     for site_index in range(site_cores.shape[0]):
-        sample_rows = lax.all_gather(current, "outb", axis=1, tiled=True)
+        x = current
+        ways, here, step = (lax.axis_size("outb"), lax.axis_index("outb"), x.shape[1])
+        dims = [n * ways if d == 1 else n for d, n in enumerate(x.shape)]
+        full = lax.dynamic_update_slice_in_dim(jnp.zeros(dims, x.dtype), x, here * step, axis=1)
+        for far in range(1, ways):
+            x = lax.ppermute(x, "outb", [(d, (d + 1) % ways) for d in range(ways)])
+            full = lax.dynamic_update_slice_in_dim(full, x, (here - far) % ways * step, axis=1)
+        sample_rows = full
         own_cols = lax.all_to_all(sample_rows, "inb", split_axis=1, concat_axis=0, tiled=True)
         partial_terms = jnp.einsum(
             "sc,pcd->psd", own_cols, site_cores[site_index], precision=lax.Precision.HIGHEST

time: 556 us -> 597 us (1.074)
  waiting for transfers between devices: 261 us -> 298 us
  local copies, waits for them, and re-layouts: 16.5 us -> 36.5 us
  blocking collectives: 138 us -> 122 us
    ppermute x0 -> x14, waiting for transfers between devices: none -> 127 us  [on_device(): x = lax.ppermute(x, 'outb', [(d, (d + 1) % ways) for d in range(ways)])]
    all_gather x2 -> x0, waiting for transfers between devices: 94.3 us -> none  [on_device(): sample_rows = lax.all_gather(current, 'outb', axis=1, tiled=True)]
    all_to_all x2, blocking collectives: 106 us -> 89.1 us  [on_device(): lax.all_to_all(sample_rows, 'inb', split_axis=1, concat_axis=0, tiled=True)]
    dynamic_update_slice x0 -> x16, local copies, waits for them, and re-layouts: none -> 9.18 us  [the longest x14 8.31 us: on_device(): lax.dynamic_update_slice_in_dim(full, x, (here - far) % ways * step, axis=1)]
    ppermute x0 -> x7, local copies, waits for them, and re-layouts: none -> 7.57 us  [on_device(): x = lax.ppermute(x, 'outb', [(d, (d + 1) % ways) for d in range(ways)])]
  transfers between devices with their start and end apart: 4 -> 16, of which waited for: 4 -> 16; matrix products, arithmetic and copies ran while one was open for 0% -> 3% of each run, Pallas kernels for 0% -> 0%
where the time goes in v1:
time: 597 us; the launch traced here: 596 us
  waiting for transfers between devices  298 us (50%)
  blocking collectives  122 us (20%)
  matrix products  119 us (20%)
  local copies, waits for them, and re-layouts  36.5 us (6%)
  between operations  14.3 us (2%)
  other arithmetic  6.19 us (1%)
    reduce_scatter x2, waiting for transfers between devices, on_device(): lax.psum_scatter(partial_terms, 'inb', scatter_dimension=1, tiled=True)  171 us
    ppermute x14, waiting for transfers between devices, on_device(): x = lax.ppermute(x, 'outb', [(d, (d + 1) % ways) for d in range(ways)])  127 us
    dot_general x2, matrix products, on_device(): jnp.einsum('sc,pcd->psd', own_cols, site_cores[site_index], precision=lax...  119 us
    all_to_all x2, blocking collectives, on_device(): lax.all_to_all(sample_rows, 'inb', split_axis=1, concat_axis=0, tiled=True)  89.1 us
    psum x2, blocking collectives, on_device(): totals = lax.psum(squares, 'outb')  32.4 us
  transfers between devices with their start and end apart: 16, of which 16 were waited for; matrix products, arithmetic and copies ran while one was open for 3% of the time, Pallas kernels for 0%

profile of v1, /device:TPU:0, one launch (start us, length us, event | category | flops | bytes accessed | tf_op | source)
XLA Modules:
  0.0 596.0 jit_solution(8416400622129177261)
XLA Ops:
  7.2 1.5 copy-done
  9.5 10.9 %collective-permute-done = f32[128,1024]{0,1:T(8,128)S(1)} collective-permute-done((f32[128,1024]{0,1:T(8,128)S(1)}, f32[128,1024]{0,1:T(8,128)S(1)}, u32[]{:S(2)}, u32[]{:S(2)}) %collective-permute-start) | collective-permute-done | bytes 524320 | tf_op jit(solution)/shard_map/ppermute | solution.py:28
  20.4 10.4 %collective-permute-done.1 = f32[128,1024]{0,1:T(8,128)S(1)} collective-permute-done((f32[128,1024]{0,1:T(8,128)S(1)}, f32[128,1024]{0,1:T(8,128)S(1)}, u32[]{:S(2)}, u32[]{:S(2)}) %collective-permute-start.1) | collective-permute-done | bytes 524320 | tf_op jit(solution)/shard_map/ppermute | solution.py:28
  30.8 10.4 %collective-permute-done.2 = f32[128,1024]{0,1:T(8,128)S(1)} collective-permute-done((f32[128,1024]{0,1:T(8,128)S(1)}, f32[128,1024]{0,1:T(8,128)S(1)}, u32[]{:S(2)}, u32[]{:S(2)}) %collective-permute-start.2) | collective-permute-done | bytes 524320 | tf_op jit(solution)/shard_map/ppermute | solution.py:28
  42.0 9.6 %collective-permute-done.3 = f32[128,1024]{0,1:T(8,128)S(1)} collective-permute-done((f32[128,1024]{0,1:T(8,128)S(1)}, f32[128,1024]{0,1:T(8,128)S(1)}, u32[]{:S(2)}, u32[]{:S(2)}) %collective-permute-start.3) | collective-permute-done | bytes 524320 | tf_op jit(solution)/shard_map/ppermute | solution.py:28
  51.7 0.8 copy-done.10
  52.5 10.5 %collective-permute-done.4 = f32[128,1024]{0,1:T(8,128)} collective-permute-done((f32[128,1024]{0,1:T(8,128)S(1)}, f32[128,1024]{0,1:T(8,128)}, u32[]{:S(2)}, u32[]{:S(2)}) %collective-permute-start.4) | collective-permute-done | bytes 524320 | tf_op jit(solution)/shard_map/ppermute | solution.py:28
  64.0 9.6 %collective-permute-done.5 = f32[128,1024]{0,1:T(8,128)} collective-permute-done((f32[128,1024]{0,1:T(8,128)}, f32[128,1024]{0,1:T(8,128)}, u32[]{:S(2)}, u32[]{:S(2)}) %collective-permute-start.5) | collective-permute-done | bytes 524320 | tf_op jit(solution)/shard_map/ppermute | solution.py:28
  73.8 1.1 constant_dynamic-update-slice_fusion.10
  74.9 1.1 constant_dynamic-update-slice_fusion.9
  76.0 8.3 %collective-permute-done.6 = f32[128,1024]{0,1:T(8,128)S(1)} collective-permute-done((f32[128,1024]{0,1:T(8,128)}, f32[128,1024]{0,1:T(8,128)S(1)}, u32[]{:S(2)}, u32[]{:S(2)}) %collective-permute-start.6) | collective-permute-done | bytes 524320 | tf_op jit(solution)/shard_map/ppermute | solution.py:28
  84.3 43.6 %all_to_all.38 = f32[128,4,2048]{0,2,1:T(8,128)} all-to-all(f32[128,4,2048]{0,2,1:T(8,128)S(1)} %bitcast.42), channel_id=1, replica_groups=mesh['inb'=4,'outb'=8] {'inb'}, dimensions={1} | all-to-all | bytes 8388608 | tf_op jit(solution)/shard_map/all_to_all | solution.py:31
  128.0 5.4 copy.10
  133.3 59.3 %fusion.6 = f32[4,512,1024]{2,1,0:T(8,128)} fusion(f32[512,2048,1]{1,0,2:T(8,128)} %bitcast.45, f32[2,4,2048,1024]{3,2,1,0:T(8,128)} %param.3), kind=kOutput, calls=%fused_computation.6 | convolution fusion | flops 51539607552 | bytes 46137344 | tf_op jit(solution)/shard_map/sc,pcd->psd/dot_general | solution.py:32
  193.4 82.4 %reduce-scatter.3.cloned.1.call-done = f32[4,128,1024]{2,1,0:T(8,128)} async-done(((f32[4,512,1024]{2,1,0:T(8,128)}), f32[4,128,1024]{2,1,0:T(8,128)}) %reduce-scatter.3.cloned.1.call-update) | async-done | bytes 2097168 | tf_op jit(solution)/shard_map/reduce_scatter | solution.py:35
  275.9 2.0 multiply_reduce_fusion.2
  277.9 16.2 %psum.14 = f32[4,128]{1,0:T(4,128)S(1)} all-reduce(f32[4,128]{1,0:T(4,128)S(1)} %get-tuple-element.5), channel_id=1, replica_groups=mesh['inb'=4,'outb'=8] {'outb'}, use_global_device_ids=true, to_apply=%region_3.4 | all-reduce | flops 512 | bytes 4096 | tf_op jit(solution)/shard_map/psum | solution.py:37
  294.3 10.4 %collective-permute-done.7 = f32[128,1024]{1,0:T(8,128)S(1)} collective-permute-done((f32[128,1024]{1,0:T(8,128)S(1)}, f32[128,1024]{1,0:T(8,128)S(1)}, u32[]{:S(2)}, u32[]{:S(2)}) %collective-permute-start.7) | collective-permute-done | bytes 524320 | tf_op jit(solution)/shard_map/ppermute | solution.py:28
  304.7 0.8 copy-done.4
  305.4 9.6 %collective-permute-done.8 = f32[128,1024]{1,0:T(8,128)S(1)} collective-permute-done((f32[128,1024]{1,0:T(8,128)S(1)}, f32[128,1024]{1,0:T(8,128)S(1)}, u32[]{:S(2)}, u32[]{:S(2)}) %collective-permute-start.8) | collective-permute-done | bytes 524320 | tf_op jit(solution)/shard_map/ppermute | solution.py:28
  315.1 0.8 copy-done.5
  315.9 9.6 %collective-permute-done.9 = f32[128,1024]{1,0:T(8,128)S(1)} collective-permute-done((f32[128,1024]{1,0:T(8,128)S(1)}, f32[128,1024]{1,0:T(8,128)S(1)}, u32[]{:S(2)}, u32[]{:S(2)}) %collective-permute-start.9) | collective-permute-done | bytes 524320 | tf_op jit(solution)/shard_map/ppermute | solution.py:28
  325.5 10.4 %collective-permute-done.10 = f32[128,1024]{1,0:T(8,128)S(1)} collective-permute-done((f32[128,1024]{1,0:T(8,128)S(1)}, f32[128,1024]{1,0:T(8,128)S(1)}, u32[]{:S(2)}, u32[]{:S(2)}) %collective-permute-start.10) | collective-permute-done | bytes 524320 | tf_op jit(solution)/shard_map/ppermute | solution.py:28
  335.9 10.5 %collective-permute-done.11 = f32[128,1024]{1,0:T(8,128)} collective-permute-done((f32[128,1024]{1,0:T(8,128)S(1)}, f32[128,1024]{1,0:T(8,128)}, u32[]{:S(2)}, u32[]{:S(2)}) %collective-permute-start.11) | collective-permute-done | bytes 524320 | tf_op jit(solution)/shard_map/ppermute | solution.py:28
  346.6 2.2 broadcast.45
  348.8 0.8 constant_dynamic-update-slice_fusion.7
  349.7 1.2 copy.12
  350.9 0.9 constant_dynamic-update-slice_fusion.6
  351.8 1.2 copy.13
  353.0 4.1 collective-permute-done.12
  357.1 0.8 constant_dynamic-update-slice_fusion.5
  358.1 0.8 constant_dynamic-update-slice_fusion.4
  359.0 1.2 copy.15
  360.2 0.8 constant_dynamic-update-slice_fusion.3
  361.1 1.2 copy.16
  362.3 0.8 constant_dynamic-update-slice_fusion.2
  363.1 1.2 copy.17
  364.4 0.9 constant_dynamic-update-slice_fusion.1
  365.2 2.6 collective-permute-done.13
  367.8 1.2 copy.18
  369.1 0.9 constant_dynamic-update-slice_fusion
  369.9 45.5 %all_to_all.39 = f32[128,4,2048]{0,2,1:T(8,128)} all-to-all(f32[128,4,2048]{0,2,1:T(8,128)} %bitcast.8), channel_id=1, replica_groups=mesh['inb'=4,'outb'=8] {'inb'}, dimensions={1} | all-to-all | bytes 8388608 | tf_op jit(solution)/shard_map/all_to_all | solution.py:31
  415.4 5.4 copy.19
  420.8 59.3 %fusion.9 = f32[4,512,1024]{2,1,0:T(8,128)} fusion(f32[512,2048,1]{1,0,2:T(8,128)} %bitcast.46, f32[2,4,2048,1024]{3,2,1,0:T(8,128)} %param.3), kind=kOutput, calls=%fused_computation.7 | convolution fusion | flops 51539607552 | bytes 46137344 | tf_op jit(solution)/shard_map/sc,pcd->psd/dot_general | solution.py:32
  480.1 88.8 %reduce-scatter.5.cloned.1.call-done = f32[4,128,1024]{2,1,0:T(8,128)} async-done(((f32[4,512,1024]{2,1,0:T(8,128)}), f32[4,128,1024]{2,1,0:T(8,128)}) %reduce-scatter.5.cloned.1.call-update) | async-done | bytes 2097168 | tf_op jit(solution)/shard_map/reduce_scatter | solution.py:35
  568.9 2.0 multiply_reduce_fusion
  570.9 16.2 %psum.15 = f32[4,128]{1,0:T(4,128)S(1)} all-reduce(f32[4,128]{1,0:T(4,128)S(1)} %get-tuple-element.3), channel_id=1, replica_groups=mesh['inb'=4,'outb'=8] {'outb'}, use_global_device_ids=true, to_apply=%region_8.9 | all-reduce | flops 512 | bytes 4096 | tf_op jit(solution)/shard_map/psum | solution.py:37
  588.3 0.9 broadcast_multiply_fusion
  (61 shorter events, 5.4 us)
Async XLA Ops:
  7.2 1.6 copy-start
  7.2 268.7 %reduce-scatter.3.cloned.1.call-start = ((), (), s32[]{:S(2)}) async-start(), calls=%async_computation.4 | async-start | bytes 10485760 | tf_op jit(solution)/shard_map/reduce_scatter | solution.py:35
  9.0 11.4 %collective-permute-start = (f32[128,1024]{0,1:T(8,128)S(1)}, f32[128,1024]{0,1:T(8,128)S(1)}, u32[]{:S(2)}, u32[]{:S(2)}) collective-permute-start(f32[128,1024]{0,1:T(8,128)S(1)} %copy.20), channel_id=1, source_target_pairs={{0,1},{1,2},{2,3},{3,4},{4,5},{5,6},{6,7},{7,0},{8,9},{9,10},{10,1... | collective-permute-start | bytes 1572872 | tf_op jit(solution)/shard_map/ppermute | solution.py:28
  20.4 20.8 %copy-start.6 = (f32[128,1024]{0,1:T(8,128)}, f32[128,1024]{0,1:T(8,128)S(1)}, u32[]{:S(2)}) copy-start(f32[128,1024]{0,1:T(8,128)S(1)} %collective-permute-done) | copy-start | bytes 1572868
  20.4 10.4 %collective-permute-start.1 = (f32[128,1024]{0,1:T(8,128)S(1)}, f32[128,1024]{0,1:T(8,128)S(1)}, u32[]{:S(2)}, u32[]{:S(2)}) collective-permute-start(f32[128,1024]{0,1:T(8,128)S(1)} %collective-permute-done), channel_id=1, source_target_pairs={{0,1},{1,2},{2,3},{3,4},{4,5},{5,6},{6,7},{7,0},{8,9},{9,10},{10,1... | collective-permute-start | bytes 1572872 | tf_op jit(solution)/shard_map/ppermute | solution.py:28
  30.8 10.4 %collective-permute-start.2 = (f32[128,1024]{0,1:T(8,128)S(1)}, f32[128,1024]{0,1:T(8,128)S(1)}, u32[]{:S(2)}, u32[]{:S(2)}) collective-permute-start(f32[128,1024]{0,1:T(8,128)S(1)} %collective-permute-done.1), channel_id=1, source_target_pairs={{0,1},{1,2},{2,3},{3,4},{4,5},{5,6},{6,7},{7,0},{8,9},{9,10},{10,1... | collective-permute-start | bytes 1572872 | tf_op jit(solution)/shard_map/ppermute | solution.py:28
  41.2 0.8 copy-start.8
  41.2 10.4 %collective-permute-start.3 = (f32[128,1024]{0,1:T(8,128)S(1)}, f32[128,1024]{0,1:T(8,128)S(1)}, u32[]{:S(2)}, u32[]{:S(2)}) collective-permute-start(f32[128,1024]{0,1:T(8,128)S(1)} %collective-permute-done.2), channel_id=1, source_target_pairs={{0,1},{1,2},{2,3},{3,4},{4,5},{5,6},{6,7},{7,0},{8,9},{9,10},{10,1... | collective-permute-start | bytes 1572872 | tf_op jit(solution)/shard_map/ppermute | solution.py:28
  51.7 0.8 copy-start.10
  52.5 10.5 %collective-permute-start.4 = (f32[128,1024]{0,1:T(8,128)S(1)}, f32[128,1024]{0,1:T(8,128)}, u32[]{:S(2)}, u32[]{:S(2)}) collective-permute-start(f32[128,1024]{0,1:T(8,128)S(1)} %collective-permute-done.3), channel_id=1, source_target_pairs={{0,1},{1,2},{2,3},{3,4},{4,5},{5,6},{6,7},{7,0},{8,9},{9,10},{10,1... | collective-permute-start | bytes 1572872 | tf_op jit(solution)/shard_map/ppermute | solution.py:28
  63.0 10.7 %collective-permute-start.5 = (f32[128,1024]{0,1:T(8,128)}, f32[128,1024]{0,1:T(8,128)}, u32[]{:S(2)}, u32[]{:S(2)}) collective-permute-start(f32[128,1024]{0,1:T(8,128)} %collective-permute-done.4), channel_id=1, source_target_pairs={{0,1},{1,2},{2,3},{3,4},{4,5},{5,6},{6,7},{7,0},{8,9},{9,10},{10,1... | collective-permute-start | bytes 1572872 | tf_op jit(solution)/shard_map/ppermute | solution.py:28
  63.0 1.0 copy-start.7
  63.0 10.8 %copy-start.9 = (f32[128,1024]{0,1:T(8,128)S(1)}, f32[128,1024]{0,1:T(8,128)}, u32[]{:S(2)}) copy-start(f32[128,1024]{0,1:T(8,128)} %copy-done.8) | copy-start | bytes 1572868
  63.0 10.8 %copy-start.11 = (f32[128,1024]{0,1:T(8,128)S(1)}, f32[128,1024]{0,1:T(8,128)}, u32[]{:S(2)}) copy-start(f32[128,1024]{0,1:T(8,128)} %copy-done.10) | copy-start | bytes 1572868
  73.7 10.6 %collective-permute-start.6 = (f32[128,1024]{0,1:T(8,128)}, f32[128,1024]{0,1:T(8,128)S(1)}, u32[]{:S(2)}, u32[]{:S(2)}) collective-permute-start(f32[128,1024]{0,1:T(8,128)} %collective-permute-done.5), channel_id=1, source_target_pairs={{0,1},{1,2},{2,3},{3,4},{4,5},{5,6},{6,7},{7,0},{8,9},{9,10},{10,1... | collective-permute-start | bytes 1572872 | tf_op jit(solution)/shard_map/ppermute | solution.py:28
  192.7 376.3 %reduce-scatter.5.cloned.1.call-start = ((), (), s32[]{:S(2)}) async-start(), calls=%async_computation.5 | async-start | bytes 10485760 | tf_op jit(solution)/shard_map/reduce_scatter | solution.py:35
  294.2 10.5 %collective-permute-start.7 = (f32[128,1024]{1,0:T(8,128)S(1)}, f32[128,1024]{1,0:T(8,128)S(1)}, u32[]{:S(2)}, u32[]{:S(2)}) collective-permute-start(f32[128,1024]{1,0:T(8,128)S(1)} %broadcast_multiply_fusion.1), channel_id=1, source_target_pairs={{0,1},{1,2},{2,3},{3,4},{4,5},{5,6},{6,7},{7,0},{8,9},{9,10},{10,1... | collective-permute-start | bytes 1572872 | tf_op jit(solution)/shard_map/ppermute | solution.py:28
  304.6 0.8 copy-start.4
  304.7 10.4 %collective-permute-start.8 = (f32[128,1024]{1,0:T(8,128)S(1)}, f32[128,1024]{1,0:T(8,128)S(1)}, u32[]{:S(2)}, u32[]{:S(2)}) collective-permute-start(f32[128,1024]{1,0:T(8,128)S(1)} %collective-permute-done.7), channel_id=1, source_target_pairs={{0,1},{1,2},{2,3},{3,4},{4,5},{5,6},{6,7},{7,0},{8,9},{9,10},{10,1... | collective-permute-start | bytes 1572872 | tf_op jit(solution)/shard_map/ppermute | solution.py:28
  315.1 0.8 copy-start.5
  315.1 10.4 %collective-permute-start.9 = (f32[128,1024]{1,0:T(8,128)S(1)}, f32[128,1024]{1,0:T(8,128)S(1)}, u32[]{:S(2)}, u32[]{:S(2)}) collective-permute-start(f32[128,1024]{1,0:T(8,128)S(1)} %collective-permute-done.8), channel_id=1, source_target_pairs={{0,1},{1,2},{2,3},{3,4},{4,5},{5,6},{6,7},{7,0},{8,9},{9,10},{10,1... | collective-permute-start | bytes 1572872 | tf_op jit(solution)/shard_map/ppermute | solution.py:28
  325.5 20.9 %copy-start.1 = (f32[128,1024]{1,0:T(8,128)}, f32[128,1024]{1,0:T(8,128)S(1)}, u32[]{:S(2)}) copy-start(f32[128,1024]{1,0:T(8,128)S(1)} %collective-permute-done.9) | copy-start | bytes 1572868
  325.5 10.4 %collective-permute-start.10 = (f32[128,1024]{1,0:T(8,128)S(1)}, f32[128,1024]{1,0:T(8,128)S(1)}, u32[]{:S(2)}, u32[]{:S(2)}) collective-permute-start(f32[128,1024]{1,0:T(8,128)S(1)} %collective-permute-done.9), channel_id=1, source_target_pairs={{0,1},{1,2},{2,3},{3,4},{4,5},{5,6},{6,7},{7,0},{8,9},{9,10},{10,1... | collective-permute-start | bytes 1572872 | tf_op jit(solution)/shard_map/ppermute | solution.py:28
  335.9 10.5 %copy-start.3 = (f32[128,1024]{1,0:T(8,128)}, f32[128,1024]{1,0:T(8,128)S(1)}, u32[]{:S(2)}) copy-start(f32[128,1024]{1,0:T(8,128)S(1)} %collective-permute-done.10) | copy-start | bytes 1572868
  335.9 10.5 %collective-permute-start.11 = (f32[128,1024]{1,0:T(8,128)S(1)}, f32[128,1024]{1,0:T(8,128)}, u32[]{:S(2)}, u32[]{:S(2)}) collective-permute-start(f32[128,1024]{1,0:T(8,128)S(1)} %collective-permute-done.10), channel_id=1, source_target_pairs={{0,1},{1,2},{2,3},{3,4},{4,5},{5,6},{6,7},{7,0},{8,9},{9,10},{10,1... | collective-permute-start | bytes 1572872 | tf_op jit(solution)/shard_map/ppermute | solution.py:28
  346.4 10.7 %collective-permute-start.12 = (f32[128,1024]{1,0:T(8,128)}, f32[128,1024]{1,0:T(8,128)}, u32[]{:S(2)}, u32[]{:S(2)}) collective-permute-start(f32[128,1024]{1,0:T(8,128)} %collective-permute-done.11), channel_id=1, source_target_pairs={{0,1},{1,2},{2,3},{3,4},{4,5},{5,6},{6,7},{7,0},{8,9},{9,10},{10,1... | collective-permute-start | bytes 1572872 | tf_op jit(solution)/shard_map/ppermute | solution.py:28
  346.6 11.3 %copy-start.2 = (f32[128,1024]{1,0:T(8,128)S(1)}, f32[128,1024]{1,0:T(8,128)}, u32[]{:S(2)}) copy-start(f32[128,1024]{1,0:T(8,128)} %copy-done.1) | copy-start | bytes 1572868
  357.1 10.7 %collective-permute-start.13 = (f32[128,1024]{1,0:T(8,128)}, f32[128,1024]{1,0:T(8,128)}, u32[]{:S(2)}, u32[]{:S(2)}) collective-permute-start(f32[128,1024]{1,0:T(8,128)} %collective-permute-done.12), channel_id=1, source_target_pairs={{0,1},{1,2},{2,3},{3,4},{4,5},{5,6},{6,7},{7,0},{8,9},{9,10},{10,1... | collective-permute-start | bytes 1572872 | tf_op jit(solution)/shard_map/ppermute | solution.py:28
Sparse Core Ops, SparseCore 0:
  192.8 83.0 reduce-scatter.2
  480.2 88.6 reduce-scatter.4
